TPU v7x, 32 devices: a whole 2x2x4 slice. The times are simulated.
32 devices in a mesh: row: 8 (over z, y), col: 2 (over core), layer: 2 (over x).
Axes of the slice: x: 2, y: 2, z: 4, core: 2. Of those that a mesh axis runs over, the one named last changes fastest.
Arguments:
- matrix: float32 [1, 8, 256, 4, 2, 256], P(None, 'row', None, None, 'col'), may hold values from -8 to 113.137085, as said below
Outputs:
- factored: float32 [1, 8, 256, 4, 2, 256], P(None, 'row', None, 'layer', 'col')
Inputs may be any that keep to these rules, and one draw needn't show every extreme that they name: `matrix`: viewed as in the first step it is symmetric, its leading 2 * 256 x 2 * 256 block is positive definite, and its diagonal entries lie between 2.5 and 5 times the square root of 512.
All inputs are finite; a program needn't handle non-finite values.
Results may differ from a plain program's by a relative error of at most 0.000059.
Values sent between devices are 32-bit elements; how exact they have to be, the bound alone decides.
No kernel may reach another device: no remote copies, remote signals or barrier semaphores. Data moves between devices by JAX's collectives and lax.ppermute only.
A program may use at most 128 MiB of HBM per device.

v0:
```python
import jax
import jax.numpy as jnp
from jax import lax
from jax.sharding import PartitionSpec as P

HIGH = lax.Precision.HIGHEST


def from_root(shard, axis, root):
    mine = lax.axis_index(axis) == root
    return lax.psum(jnp.where(mine, shard, jnp.zeros_like(shard)), axis)


def factor_block(diag_block):
    lower_fac = jnp.linalg.cholesky(diag_block)
    identity = jnp.eye(diag_block.shape[0], dtype=jnp.float32)
    inverse = lax.linalg.triangular_solve(lower_fac, identity, left_side=True, lower=True)
    return (lower_fac, inverse)


def on_device(matrix):
    row_total = lax.axis_size("row")
    col_total = lax.axis_size("col")
    layer_total = lax.axis_size("layer")
    grid_row = lax.axis_index("row")
    grid_col = lax.axis_index("col")
    grid_layer = lax.axis_index("layer")
    row_blocks = matrix.shape[0]
    block_size = matrix.shape[2]
    col_blocks = matrix.shape[3]
    half = block_size // layer_total
    owned = col_blocks // layer_total
    rows = row_blocks * block_size
    tile = matrix.reshape(rows, col_blocks * block_size)
    row_ids = jnp.arange(rows) // block_size * row_total + grid_row
    column = tile[:, :block_size]
    pending = None
    total = None
    panels = []
    for section in range(2):
        diag_block = from_root(column, "row", section % row_total)
        lower_fac, inverse = factor_block(diag_block)
        solved = jnp.dot(column, inverse.T, precision=HIGH, preferred_element_type=jnp.float32)
        repeated = jnp.tile(lower_fac, (row_blocks, 1))
        complete = jnp.where(
            row_ids[:, None] > section,
            solved,
            jnp.where(row_ids[:, None] == section, repeated, 0.0),
        )
        panels.append(complete)
        share = lax.dynamic_slice_in_dim(complete, grid_layer * half, half, 1)
        share = from_root(share, "col", section % col_total)
        gathered = lax.all_gather(
            share.reshape(row_blocks, 1, block_size, half), "row", axis=1, tiled=True
        )
        grouped = gathered.reshape(col_blocks, col_total, block_size, half)
        picked = lax.dynamic_index_in_dim(grouped, grid_col, 1, keepdims=False).reshape(
            col_blocks * block_size, half
        )
        update = lax.dot_general(
            share,
            picked,
            (((1,), (1,)), ((), ())),
            precision=HIGH,
            preferred_element_type=jnp.float32,
        )
        if section == 0:
            head = lax.psum(update[:, :block_size], "layer")
            column = tile[:, :block_size] - head
            pending = update
        else:
            total = pending + update
    reduced = lax.psum_scatter(
        total.reshape(rows, col_blocks, block_size), "layer", scatter_dimension=1, tiled=True
    )
    own_part = (
        lax.dynamic_slice_in_dim(
            tile.reshape(rows, col_blocks, block_size), grid_layer * owned, owned, 1
        )
        - reduced
    )
    replacement = jnp.where(grid_col == 0, panels[0], panels[1])
    global_ids = (grid_layer * owned + jnp.arange(owned)) * col_total + grid_col
    result = jnp.where((global_ids < 2)[None, :, None], replacement[:, None, :], own_part)
    return result.reshape(row_blocks, 1, block_size, owned, 1, block_size)


def solution(mesh):
    in_specs = (P(None, "row", None, None, "col", None),)
    out_specs = P(None, "row", None, "layer", "col", None)
    return jax.shard_map(
        on_device, mesh=mesh, in_specs=in_specs, out_specs=out_specs, check_vma=False
    )
```

profile of v0, /device:TPU:0, one launch (start us, length us, event | category | flops | bytes accessed | tf_op | source)
XLA Modules:
  0.0 472.5 jit_solution(6674159370767984335)
XLA Ops:
  6.5 2.3 copy.16
  9.8 74.7 %all-reduce.7.cloned.1.call-done = f32[256,256]{0,1:T(8,128)} async-done(((f32[256,256]{0,1:T(8,128)}), f32[256,256]{0,1:T(8,128)}) %all-reduce.7.cloned.1.call-update) | async-done | bytes 262160 | tf_op jit(solution)/shard_map/psum | solution.py:11
  85.7 11.7 %cholesky.130 = f32[128,128]{1,0:T(8,128)S(1)} custom-call(f32[128,128]{1,0:T(8,128)S(1)} %cholesky.194), custom_call_target="Cholesky" | custom-call | tf_op jit(solution)/shard_map/jit(cholesky)/cholesky | solution.py:15
  97.4 9.8 %custom-call.13 = f32[1,128,128]{1,2,0:T(8,128)S(1)} custom-call(f32[1,128,128]{2,1,0:T(8,128)S(1)} %get-tuple-element.62), custom_call_target="InvertDiagBlocksLowerTriangular" | custom-call | tf_op jit(solution)/shard_map/jit(cholesky)/cholesky | solution.py:15
  107.7 11.7 %cholesky.147 = f32[128,128]{1,0:T(8,128)S(1)} custom-call(f32[128,128]{1,0:T(8,128)S(1)} %convolution_subtract_fusion.3), custom_call_target="Cholesky" | custom-call | tf_op jit(solution)/shard_map/jit(cholesky)/cholesky | solution.py:15
  122.0 4.8 %while.4 = (s32[]{:T(128)}, f32[256,256]{0,1:T(8,128)S(1)}, s32[2,2]{1,0:T(2,128)S(1)}, f32[2,128,128]{2,1,0:T(8,128)S(1)}, s32[]{:T(128)}) while((s32[]{:T(128)}, f32[256,256]{0,1:T(8,128)S(1)}, s32[2,2]{1,0:T(2,128)S(1)}, f32[2,128,128]{2,1,0:T(8,128)S(1)}, s32[]{:T(128)}) %tuple.46), condition=%wide.while_cond, body=%wide.while_body.sunk | while | flops 2 | bytes 393321 | solution.py:17
  126.8 19.7 %custom-call.14 = f32[2,128,128]{1,2,0:T(8,128)S(1)} custom-call(f32[2,128,128]{2,1,0:T(8,128)S(1)} %get-tuple-element.21), custom_call_target="InvertDiagBlocksLowerTriangular" | custom-call | tf_op jit(solution)/shard_map/triangular_solve/custom-call.0 | solution.py:17
  148.6 17.2 %all-reduce.9.cloned.1.call-done = f32[256,128]{0,1:T(8,128)} async-done(((f32[256,128]{0,1:T(8,128)}), f32[256,128]{0,1:T(8,128)}) %all-reduce.9.cloned.1.call-update) | async-done | bytes 131088 | tf_op jit(solution)/shard_map/psum | solution.py:11
  165.9 42.6 %all-gather.5.cloned.1.call-done = f32[2048,128]{0,1:T(8,128)} async-done(((f32[256,128]{0,1:T(8,128)}), f32[2048,128]{0,1:T(8,128)}) %all-gather.5.cloned.1.call-update) | async-done | bytes 1048592 | tf_op jit(solution)/shard_map/all_gather | solution.py:53
  208.5 2.1 reshape.86
  210.6 1.6 dynamic-slice_reduce_fusion.1
  215.1 22.4 %all-reduce.11.cloned.1.call-done = f32[256,256]{0,1:T(8,128)} async-done(((f32[256,256]{0,1:T(8,128)}), f32[256,256]{0,1:T(8,128)}) %all-reduce.11.cloned.1.call-update) | async-done | bytes 262160 | tf_op jit(solution)/shard_map/psum | solution.py:68
  237.5 1.7 broadcast_select_fusion
  239.5 72.3 %all-reduce.13.cloned.1.call-done = f32[256,256]{0,1:T(8,128)} async-done(((f32[256,256]{0,1:T(8,128)}), f32[256,256]{0,1:T(8,128)}) %all-reduce.13.cloned.1.call-update) | async-done | bytes 262160 | tf_op jit(solution)/shard_map/psum | solution.py:11
  313.0 11.7 %cholesky.164 = f32[128,128]{1,0:T(8,128)S(1)} custom-call(f32[128,128]{1,0:T(8,128)S(1)} %cholesky.197), custom_call_target="Cholesky" | custom-call | tf_op jit(solution)/shard_map/jit(cholesky)/cholesky | solution.py:15
  324.8 9.8 %custom-call.15 = f32[1,128,128]{1,2,0:T(8,128)S(1)} custom-call(f32[1,128,128]{2,1,0:T(8,128)S(1)} %get-tuple-element.60), custom_call_target="InvertDiagBlocksLowerTriangular" | custom-call | tf_op jit(solution)/shard_map/jit(cholesky)/cholesky | solution.py:15
  335.1 11.7 %cholesky.181 = f32[128,128]{1,0:T(8,128)S(1)} custom-call(f32[128,128]{1,0:T(8,128)S(1)} %convolution_subtract_fusion.2), custom_call_target="Cholesky" | custom-call | tf_op jit(solution)/shard_map/jit(cholesky)/cholesky | solution.py:15
  349.8 4.4 while.5
  354.2 19.7 %custom-call.16 = f32[2,128,128]{1,2,0:T(8,128)S(1)} custom-call(f32[2,128,128]{2,1,0:T(8,128)S(1)} %get-tuple-element.22), custom_call_target="InvertDiagBlocksLowerTriangular" | custom-call | tf_op jit(solution)/shard_map/triangular_solve/custom-call.0 | solution.py:17
  376.7 17.2 %all-reduce.15.cloned.1.call-done = f32[256,128]{0,1:T(8,128)} async-done(((f32[256,128]{0,1:T(8,128)}), f32[256,128]{0,1:T(8,128)}) %all-reduce.15.cloned.1.call-update) | async-done | bytes 131088 | tf_op jit(solution)/shard_map/psum | solution.py:11
  393.9 42.6 %all-gather.7.cloned.1.call-done = f32[2048,128]{0,1:T(8,128)} async-done(((f32[256,128]{0,1:T(8,128)}), f32[2048,128]{0,1:T(8,128)}) %all-gather.7.cloned.1.call-update) | async-done | bytes 1048592 | tf_op jit(solution)/shard_map/all_gather | solution.py:53
  436.6 2.1 reshape.89
  438.7 1.6 dynamic-slice_reduce_fusion
  445.0 17.9 %reduce-scatter.2.cloned.1.call-done = f32[256,2,256]{2,0,1:T(8,128)} async-done(((f32[256,4,256]{2,0,1:T(8,128)}), f32[256,2,256]{2,0,1:T(8,128)}) %reduce-scatter.2.cloned.1.call-update) | async-done | bytes 524304 | tf_op jit(solution)/shard_map/reduce_scatter | solution.py:73
  (109 shorter events, 30.6 us)
Async XLA Ops:
  6.5 77.9 %all-reduce.7.cloned.1.call-start = ((), (), s32[]{:S(2)}) async-start(), calls=%async_computation.1 | async-start | bytes 524288 | tf_op jit(solution)/shard_map/psum | solution.py:11
  9.6 156.2 %all-reduce.9.cloned.1.call-start = ((), (), s32[]{:S(2)}) async-start(), calls=%async_computation.2 | async-start | bytes 262144 | tf_op jit(solution)/shard_map/psum | solution.py:11
  84.4 1.2 copy-start.1
  148.5 60.0 %all-gather.5.cloned.1.call-start = ((), (), s32[]{:S(2)}) async-start(), calls=%async_computation.7 | async-start | bytes 1179648 | tf_op jit(solution)/shard_map/all_gather | solution.py:53
  165.8 71.7 %all-reduce.11.cloned.1.call-start = ((), (), s32[]{:S(2)}) async-start(), calls=%async_computation.3 | async-start | bytes 524288 | tf_op jit(solution)/shard_map/psum | solution.py:68
  212.2 0.9 copy-start.4
  215.0 96.7 %all-reduce.13.cloned.1.call-start = ((), (), s32[]{:S(2)}) async-start(), calls=%async_computation.4 | async-start | bytes 524288 | tf_op jit(solution)/shard_map/psum | solution.py:11
  239.2 154.7 %all-reduce.15.cloned.1.call-start = ((), (), s32[]{:S(2)}) async-start(), calls=%async_computation.5 | async-start | bytes 262144 | tf_op jit(solution)/shard_map/psum | solution.py:11
  311.8 1.2 copy-start.2
  374.6 1.0 copy-start.3
  376.6 59.9 %all-gather.7.cloned.1.call-start = ((), (), s32[]{:S(2)}) async-start(), calls=%async_computation.8 | async-start | bytes 1179648 | tf_op jit(solution)/shard_map/all_gather | solution.py:53
  393.9 69.0 %reduce-scatter.2.cloned.1.call-start = ((), (), s32[]{:S(2)}) async-start(), calls=%async_computation.6 | async-start | bytes 1572864 | tf_op jit(solution)/shard_map/reduce_scatter | solution.py:73
  440.3 0.9 copy-start.5
  443.3 1.2 copy-start
Sparse Core Ops, SparseCore 0:
  10.7 73.7 all-reduce.6
  148.7 17.0 all-reduce.8
  167.8 40.5 all-gather.4
  215.2 22.2 all-reduce.10
  240.7 71.0 all-reduce.12
  376.7 17.0 all-reduce.14
  395.9 40.5 all-gather.6
  443.5 19.3 reduce-scatter.1
where the time goes:
time: 481 us; the launch traced here: 472 us
  waiting for transfers between devices  307 us (64%)
  other arithmetic  113 us (23%)
  local copies, waits for them, and re-layouts  28.5 us (6%)
  between operations  16.8 us (3%)
  matrix products  5.65 us (1%)
    psum x4, waiting for transfers between devices, from_root(): return lax.psum(jnp.where(mine, shard, jnp.zeros_like(shard)), axis)  181 us
    all_gather x2, waiting for transfers between devices, on_device(): lax.all_gather(share.reshape(row_blocks, 1, block_size, half), 'row', axi...  85.2 us
    another operation x13, other arithmetic, factor_block(): lower_fac = jnp.linalg.cholesky(diag_block)  68.7 us
    another operation x5, other arithmetic, factor_block(): lax.linalg.triangular_solve(lower_fac, identity, left_side=True, lower=True)  39.4 us
    psum x1, waiting for transfers between devices, on_device(): head = lax.psum(update[:, :block_size], 'layer')  22.4 us
    reduce_scatter x1, waiting for transfers between devices, on_device(): lax.psum_scatter(total.reshape(rows, col_blocks, block_size), 'layer', sc...  17.9 us
  transfers between devices with their start and end apart: 8, of which 8 were waited for; matrix products, arithmetic and copies ran while one was open for 0% of the time, Pallas kernels for 0%

commit v1 on v0

--- a/solution.py
+++ b/solution.py
@@ -4,6 +4,24 @@
 from jax.sharding import PartitionSpec as P
 
 HIGH = lax.Precision.HIGHEST
+
+
+def ring_gather(shard, axis, dim):
+    ways, here, step = (lax.axis_size(axis), lax.axis_index(axis), shard.shape[dim])
+    dims = [n * ways if d == dim else n for d, n in enumerate(shard.shape)]
+    full = lax.dynamic_update_slice_in_dim(
+        jnp.zeros(dims, shard.dtype), shard, here * step, axis=dim
+    )
+    going_up = going_down = shard
+    for far in range(1, ways // 2 + 1):
+        going_up = lax.ppermute(going_up, axis, [(d, (d + 1) % ways) for d in range(ways)])
+        full = lax.dynamic_update_slice_in_dim(full, going_up, (here - far) % ways * step, axis=dim)
+        if 2 * far < ways:
+            going_down = lax.ppermute(going_down, axis, [(d, (d - 1) % ways) for d in range(ways)])
+            full = lax.dynamic_update_slice_in_dim(
+                full, going_down, (here + far) % ways * step, axis=dim
+            )
+    return full
 
 
 def from_root(shard, axis, root):
@@ -50,9 +68,7 @@
         panels.append(complete)
         share = lax.dynamic_slice_in_dim(complete, grid_layer * half, half, 1)
         share = from_root(share, "col", section % col_total)
-        gathered = lax.all_gather(
-            share.reshape(row_blocks, 1, block_size, half), "row", axis=1, tiled=True
-        )
+        gathered = ring_gather(share.reshape(row_blocks, 1, block_size, half), "row", 1)
         grouped = gathered.reshape(col_blocks, col_total, block_size, half)
         picked = lax.dynamic_index_in_dim(grouped, grid_col, 1, keepdims=False).reshape(
             col_blocks * block_size, half

time: 481 us -> 441 us (0.917); the launches traced: 472 us -> 441 us
  waiting for transfers between devices: 307 us -> 255 us
  starting transfers between devices: 0.46 us -> 27.9 us
  local copies, waits for them, and re-layouts: 28.5 us -> 22.1 us
    all_gather x2 -> x0, waiting for transfers between devices: 85.2 us -> none  [on_device(): lax.all_gather(share.reshape(row_blocks, 1, block_size, half), 'row', axi...]
    ppermute x0 -> x14, waiting for transfers between devices: none -> 34.4 us  [the longest x8 29.5 us: ring_gather(): lax.ppermute(going_up, axis, [(d, (d + 1) % ways) for d in range(ways)])]
    ppermute x0 -> x14, starting transfers between devices: none -> 27.6 us  [the longest x6 20.1 us: ring_gather(): lax.ppermute(going_down, axis, [(d, (d - 1) % ways) for d in range(ways)])]
  transfers between devices with their start and end apart: 8 -> 20, of which waited for: 8 -> 17; matrix products, arithmetic and copies ran while one was open for 0% -> 1% of each run, Pallas kernels for 0% -> 0%
where the time goes in v1:
time: 441 us
  waiting for transfers between devices  255 us (58%)
  other arithmetic  113 us (26%)
  starting transfers between devices  27.9 us (6%)
  local copies, waits for them, and re-layouts  22.1 us (5%)
  between operations  16.8 us (4%)
  matrix products  5.65 us (1%)
    psum x4, waiting for transfers between devices, from_root(): return lax.psum(jnp.where(mine, shard, jnp.zeros_like(shard)), axis)  182 us
    another operation x13, other arithmetic, factor_block(): lower_fac = jnp.linalg.cholesky(diag_block)  68.6 us
    another operation x5, other arithmetic, factor_block(): lax.linalg.triangular_solve(lower_fac, identity, left_side=True, lower=True)  39.4 us
    ppermute x8, waiting for transfers between devices, ring_gather(): lax.ppermute(going_up, axis, [(d, (d + 1) % ways) for d in range(ways)])  29.5 us
    psum x1, waiting for transfers between devices, on_device(): head = lax.psum(update[:, :block_size], 'layer')  22.3 us
    ppermute x6, starting transfers between devices, ring_gather(): lax.ppermute(going_down, axis, [(d, (d - 1) % ways) for d in range(ways)])  20.1 us
    reduce_scatter x1, waiting for transfers between devices, on_device(): lax.psum_scatter(total.reshape(rows, col_blocks, block_size), 'layer', sc...  16.2 us
  transfers between devices with their start and end apart: 20, of which 17 were waited for; matrix products, arithmetic and copies ran while one was open for 1% of the time, Pallas kernels for 0%

profile of v1, /device:TPU:0, one launch (start us, length us, event | category | flops | bytes accessed | tf_op | source)
XLA Modules:
  0.0 440.7 jit_solution(3799404772581854445)
XLA Ops:
  9.8 74.7 %all-reduce.7.cloned.1.call-done = f32[256,256]{0,1:T(8,128)} async-done(((f32[256,256]{0,1:T(8,128)}), f32[256,256]{0,1:T(8,128)}) %all-reduce.7.cloned.1.call-update) | async-done | bytes 262160 | tf_op jit(solution)/shard_map/psum | solution.py:29
  85.7 11.7 %cholesky.130 = f32[128,128]{1,0:T(8,128)S(1)} custom-call(f32[128,128]{1,0:T(8,128)S(1)} %cholesky.194), custom_call_target="Cholesky" | custom-call | tf_op jit(solution)/shard_map/jit(cholesky)/cholesky | solution.py:33
  97.4 9.8 %custom-call.13 = f32[1,128,128]{1,2,0:T(8,128)S(1)} custom-call(f32[1,128,128]{2,1,0:T(8,128)S(1)} %get-tuple-element.78), custom_call_target="InvertDiagBlocksLowerTriangular" | custom-call | tf_op jit(solution)/shard_map/jit(cholesky)/cholesky | solution.py:33
  107.7 11.7 %cholesky.147 = f32[128,128]{1,0:T(8,128)S(1)} custom-call(f32[128,128]{1,0:T(8,128)S(1)} %convolution_subtract_fusion.3), custom_call_target="Cholesky" | custom-call | tf_op jit(solution)/shard_map/jit(cholesky)/cholesky | solution.py:33
  122.0 4.5 %while.4 = (s32[]{:T(128)}, f32[256,256]{0,1:T(8,128)S(1)}, s32[2,2]{1,0:T(2,128)S(1)}, f32[2,128,128]{2,1,0:T(8,128)S(1)}, s32[]{:T(128)}) while((s32[]{:T(128)}, f32[256,256]{0,1:T(8,128)S(1)}, s32[2,2]{1,0:T(2,128)S(1)}, f32[2,128,128]{2,1,0:T(8,128)S(1)}, s32[]{:T(128)}) %tuple.50), condition=%wide.while_cond, body=%wide.while_body.sunk | while | flops 2 | bytes 393321 | solution.py:35
  126.5 19.7 %custom-call.14 = f32[2,128,128]{1,2,0:T(8,128)S(1)} custom-call(f32[2,128,128]{2,1,0:T(8,128)S(1)} %get-tuple-element.21), custom_call_target="InvertDiagBlocksLowerTriangular" | custom-call | tf_op jit(solution)/shard_map/triangular_solve/custom-call.0 | solution.py:35
  148.3 17.2 %all-reduce.9.cloned.1.call-done = f32[256,128]{0,1:T(8,128)} async-done(((f32[256,128]{0,1:T(8,128)}), f32[256,128]{0,1:T(8,128)}) %all-reduce.9.cloned.1.call-update) | async-done | bytes 131088 | tf_op jit(solution)/shard_map/psum | solution.py:29
  167.4 3.7 collective-permute-start.1
  171.2 3.2 collective-permute-done
  176.2 3.5 collective-permute-start.3
  183.9 3.7 collective-permute-start.5
  190.4 7.5 %collective-permute-done.6 = f32[1,1,256,128]{2,3,1,0:T(8,128)S(1)} collective-permute-done((f32[1,1,256,128]{2,3,1,0:T(8,128)S(1)}, f32[1,1,256,128]{2,3,1,0:T(8,128)S(1)}, u32[]{:S(2)}, u32[]{:S(2)}) %collective-permute-start.6) | collective-permute-done | bytes 131104 | tf_op jit(solution)/shard_map/ppermute | solution.py:17
  200.1 22.3 %all-reduce.11.cloned.1.call-done = f32[256,256]{0,1:T(8,128)} async-done(((f32[256,256]{0,1:T(8,128)}), f32[256,256]{0,1:T(8,128)}) %all-reduce.11.cloned.1.call-update) | async-done | bytes 262160 | tf_op jit(solution)/shard_map/psum | solution.py:84
  224.2 72.5 %all-reduce.13.cloned.1.call-done = f32[256,256]{0,1:T(8,128)} async-done(((f32[256,256]{0,1:T(8,128)}), f32[256,256]{0,1:T(8,128)}) %all-reduce.13.cloned.1.call-update) | async-done | bytes 262160 | tf_op jit(solution)/shard_map/psum | solution.py:29
  297.9 11.7 %cholesky.164 = f32[128,128]{1,0:T(8,128)S(1)} custom-call(f32[128,128]{1,0:T(8,128)S(1)} %cholesky.197), custom_call_target="Cholesky" | custom-call | tf_op jit(solution)/shard_map/jit(cholesky)/cholesky | solution.py:33
  309.7 9.8 %custom-call.15 = f32[1,128,128]{1,2,0:T(8,128)S(1)} custom-call(f32[1,128,128]{2,1,0:T(8,128)S(1)} %get-tuple-element.76), custom_call_target="InvertDiagBlocksLowerTriangular" | custom-call | tf_op jit(solution)/shard_map/jit(cholesky)/cholesky | solution.py:33
  320.0 11.7 %cholesky.181 = f32[128,128]{1,0:T(8,128)S(1)} custom-call(f32[128,128]{1,0:T(8,128)S(1)} %convolution_subtract_fusion.2), custom_call_target="Cholesky" | custom-call | tf_op jit(solution)/shard_map/jit(cholesky)/cholesky | solution.py:33
  334.7 4.4 %while.5 = (s32[]{:T(128)}, f32[256,256]{0,1:T(8,128)S(1)}, s32[2,2]{1,0:T(2,128)S(1)}, f32[2,128,128]{2,1,0:T(8,128)S(1)}, s32[]{:T(128)}) while((s32[]{:T(128)}, f32[256,256]{0,1:T(8,128)S(1)}, s32[2,2]{1,0:T(2,128)S(1)}, f32[2,128,128]{2,1,0:T(8,128)S(1)}, s32[]{:T(128)}) %tuple.68), condition=%wide.while_cond.clone, body=%wide.while_body.clone.sunk | while | flops 2 | bytes 393321 | solution.py:35
  339.1 19.7 %custom-call.16 = f32[2,128,128]{1,2,0:T(8,128)S(1)} custom-call(f32[2,128,128]{2,1,0:T(8,128)S(1)} %get-tuple-element.22), custom_call_target="InvertDiagBlocksLowerTriangular" | custom-call | tf_op jit(solution)/shard_map/triangular_solve/custom-call.0 | solution.py:35
  361.6 17.2 %all-reduce.15.cloned.1.call-done = f32[256,128]{0,1:T(8,128)} async-done(((f32[256,128]{0,1:T(8,128)}), f32[256,128]{0,1:T(8,128)}) %all-reduce.15.cloned.1.call-update) | async-done | bytes 131088 | tf_op jit(solution)/shard_map/psum | solution.py:29
  389.9 3.2 collective-permute-start.10
  397.8 3.1 collective-permute-start.12
  405.0 6.1 %collective-permute-done.13 = f32[1,1,256,128]{2,3,1,0:T(8,128)S(1)} collective-permute-done((f32[1,1,256,128]{2,3,1,0:T(8,128)S(1)}, f32[1,1,256,128]{2,3,1,0:T(8,128)S(1)}, u32[]{:S(2)}, u32[]{:S(2)}) %collective-permute-start.13) | collective-permute-done | bytes 131104 | tf_op jit(solution)/shard_map/ppermute | solution.py:17
  415.2 16.2 %reduce-scatter.2.cloned.1.call-done = f32[256,2,256]{2,0,1:T(8,128)} async-done(((f32[256,4,256]{2,0,1:T(8,128)}), f32[256,2,256]{2,0,1:T(8,128)}) %reduce-scatter.2.cloned.1.call-update) | async-done | bytes 524304 | tf_op jit(solution)/shard_map/reduce_scatter | solution.py:89
  (161 shorter events, 63.5 us)
Async XLA Ops:
  6.5 77.9 %all-reduce.7.cloned.1.call-start = ((), (), s32[]{:S(2)}) async-start(), calls=%async_computation.1 | async-start | bytes 524288 | tf_op jit(solution)/shard_map/psum | solution.py:29
  9.6 155.9 %all-reduce.9.cloned.1.call-start = ((), (), s32[]{:S(2)}) async-start(), calls=%async_computation.2 | async-start | bytes 262144 | tf_op jit(solution)/shard_map/psum | solution.py:29
  84.4 1.2 copy-start.1
  148.3 74.1 %all-reduce.11.cloned.1.call-start = ((), (), s32[]{:S(2)}) async-start(), calls=%async_computation.3 | async-start | bytes 524288 | tf_op jit(solution)/shard_map/psum | solution.py:84
  165.5 1.8 copy-start.4
  165.5 8.8 %collective-permute-start = (f32[1,1,256,128]{2,3,1,0:T(8,128)}, f32[1,1,256,128]{2,3,1,0:T(8,128)S(1)}, u32[]{:S(2)}, u32[]{:S(2)}) collective-permute-start(f32[1,1,256,128]{2,3,1,0:T(8,128)} %bitcast.95), channel_id=1, source_target_pairs={{0,4},{4,8},{8,12},{12,16},{16,20},{20,24},{24,28},{28,0},{1,5},{5... | collective-permute-start | bytes 393224 | tf_op jit(solution)/shard_map/ppermute | solution.py:17
  167.4 8.7 %collective-permute-start.1 = (f32[1,1,256,128]{2,3,1,0:T(8,128)S(1)}, f32[1,1,256,128]{2,3,1,0:T(8,128)S(1)}, u32[]{:S(2)}, u32[]{:S(2)}) collective-permute-start(f32[1,1,256,128]{2,3,1,0:T(8,128)S(1)} %bitcast.97), channel_id=1, source_target_pairs={{0,28},{4,0},{8,4},{12,8},{16,12},{20,16},{24,20},{28,24},{1,29},{... | collective-permute-start | bytes 393224 | tf_op jit(solution)/shard_map/ppermute | solution.py:20
  174.5 7.7 %collective-permute-start.2 = (f32[1,1,256,128]{2,3,1,0:T(8,128)S(1)}, f32[1,1,256,128]{2,3,1,0:T(8,128)S(1)}, u32[]{:S(2)}, u32[]{:S(2)}) collective-permute-start(f32[1,1,256,128]{2,3,1,0:T(8,128)S(1)} %collective-permute-done), channel_id=1, source_target_pairs={{0,4},{4,8},{8,12},{12,16},{16,20},{20,24},{24,28},{28,0},{1,5},{5... | collective-permute-start | bytes 393224 | tf_op jit(solution)/shard_map/ppermute | solution.py:17
  176.2 7.5 %collective-permute-start.3 = (f32[1,1,256,128]{2,3,1,0:T(8,128)S(1)}, f32[1,1,256,128]{2,3,1,0:T(8,128)S(1)}, u32[]{:S(2)}, u32[]{:S(2)}) collective-permute-start(f32[1,1,256,128]{2,3,1,0:T(8,128)S(1)} %collective-permute-done.1), channel_id=1, source_target_pairs={{0,28},{4,0},{8,4},{12,8},{16,12},{20,16},{24,20},{28,24},{1,29},{... | collective-permute-start | bytes 393224 | tf_op jit(solution)/shard_map/ppermute | solution.py:20
  182.3 7.8 %collective-permute-start.4 = (f32[1,1,256,128]{2,3,1,0:T(8,128)S(1)}, f32[1,1,256,128]{2,3,1,0:T(8,128)S(1)}, u32[]{:S(2)}, u32[]{:S(2)}) collective-permute-start(f32[1,1,256,128]{2,3,1,0:T(8,128)S(1)} %collective-permute-done.2), channel_id=1, source_target_pairs={{0,4},{4,8},{8,12},{12,16},{16,20},{20,24},{24,28},{28,0},{1,5},{5... | collective-permute-start | bytes 393224 | tf_op jit(solution)/shard_map/ppermute | solution.py:17
  183.9 6.4 %collective-permute-start.5 = (f32[1,1,256,128]{2,3,1,0:T(8,128)S(1)}, f32[1,1,256,128]{2,3,1,0:T(8,128)S(1)}, u32[]{:S(2)}, u32[]{:S(2)}) collective-permute-start(f32[1,1,256,128]{2,3,1,0:T(8,128)S(1)} %collective-permute-done.3), channel_id=1, source_target_pairs={{0,28},{4,0},{8,4},{12,8},{16,12},{20,16},{24,20},{28,24},{1,29},{... | collective-permute-start | bytes 393224 | tf_op jit(solution)/shard_map/ppermute | solution.py:20
  190.2 7.7 %collective-permute-start.6 = (f32[1,1,256,128]{2,3,1,0:T(8,128)S(1)}, f32[1,1,256,128]{2,3,1,0:T(8,128)S(1)}, u32[]{:S(2)}, u32[]{:S(2)}) collective-permute-start(f32[1,1,256,128]{2,3,1,0:T(8,128)S(1)} %collective-permute-done.4), channel_id=1, source_target_pairs={{0,4},{4,8},{8,12},{12,16},{16,20},{20,24},{24,28},{28,0},{1,5},{5... | collective-permute-start | bytes 393224 | tf_op jit(solution)/shard_map/ppermute | solution.py:17
  200.0 96.7 %all-reduce.13.cloned.1.call-start = ((), (), s32[]{:S(2)}) async-start(), calls=%async_computation.4 | async-start | bytes 524288 | tf_op jit(solution)/shard_map/psum | solution.py:29
  224.1 154.7 %all-reduce.15.cloned.1.call-start = ((), (), s32[]{:S(2)}) async-start(), calls=%async_computation.5 | async-start | bytes 262144 | tf_op jit(solution)/shard_map/psum | solution.py:29
  361.5 69.9 %reduce-scatter.2.cloned.1.call-start = ((), (), s32[]{:S(2)}) async-start(), calls=%async_computation.6 | async-start | bytes 1572864 | tf_op jit(solution)/shard_map/reduce_scatter | solution.py:89
  378.8 2.8 copy-start.5
  378.8 8.8 %collective-permute-start.7 = (f32[1,1,256,128]{2,3,1,0:T(8,128)}, f32[1,1,256,128]{2,3,1,0:T(8,128)S(1)}, u32[]{:S(2)}, u32[]{:S(2)}) collective-permute-start(f32[1,1,256,128]{2,3,1,0:T(8,128)} %bitcast.98), channel_id=1, source_target_pairs={{0,4},{4,8},{8,12},{12,16},{16,20},{20,24},{24,28},{28,0},{1,5},{5... | collective-permute-start | bytes 393224 | tf_op jit(solution)/shard_map/ppermute | solution.py:17
  381.6 8.2 %collective-permute-start.8 = (f32[1,1,256,128]{2,3,1,0:T(8,128)S(1)}, f32[1,1,256,128]{2,3,1,0:T(8,128)S(1)}, u32[]{:S(2)}, u32[]{:S(2)}) collective-permute-start(f32[1,1,256,128]{2,3,1,0:T(8,128)S(1)} %bitcast.100), channel_id=1, source_target_pairs={{0,28},{4,0},{8,4},{12,8},{16,12},{20,16},{24,20},{28,24},{1,29},{... | collective-permute-start | bytes 393224 | tf_op jit(solution)/shard_map/ppermute | solution.py:20
  387.7 7.7 %collective-permute-start.9 = (f32[1,1,256,128]{2,3,1,0:T(8,128)S(1)}, f32[1,1,256,128]{2,3,1,0:T(8,128)S(1)}, u32[]{:S(2)}, u32[]{:S(2)}) collective-permute-start(f32[1,1,256,128]{2,3,1,0:T(8,128)S(1)} %collective-permute-done.7), channel_id=1, source_target_pairs={{0,4},{4,8},{8,12},{12,16},{16,20},{20,24},{24,28},{28,0},{1,5},{5... | collective-permute-start | bytes 393224 | tf_op jit(solution)/shard_map/ppermute | solution.py:17
  389.9 7.8 %collective-permute-start.10 = (f32[1,1,256,128]{2,3,1,0:T(8,128)S(1)}, f32[1,1,256,128]{2,3,1,0:T(8,128)S(1)}, u32[]{:S(2)}, u32[]{:S(2)}) collective-permute-start(f32[1,1,256,128]{2,3,1,0:T(8,128)S(1)} %collective-permute-done.8), channel_id=1, source_target_pairs={{0,28},{4,0},{8,4},{12,8},{16,12},{20,16},{24,20},{28,24},{1,29},{... | collective-permute-start | bytes 393224 | tf_op jit(solution)/shard_map/ppermute | solution.py:20
  395.5 7.8 %collective-permute-start.11 = (f32[1,1,256,128]{2,3,1,0:T(8,128)S(1)}, f32[1,1,256,128]{2,3,1,0:T(8,128)S(1)}, u32[]{:S(2)}, u32[]{:S(2)}) collective-permute-start(f32[1,1,256,128]{2,3,1,0:T(8,128)S(1)} %collective-permute-done.9), channel_id=1, source_target_pairs={{0,4},{4,8},{8,12},{12,16},{16,20},{20,24},{24,28},{28,0},{1,5},{5... | collective-permute-start | bytes 393224 | tf_op jit(solution)/shard_map/ppermute | solution.py:17
  397.8 7.1 %collective-permute-start.12 = (f32[1,1,256,128]{2,3,1,0:T(8,128)S(1)}, f32[1,1,256,128]{2,3,1,0:T(8,128)S(1)}, u32[]{:S(2)}, u32[]{:S(2)}) collective-permute-start(f32[1,1,256,128]{2,3,1,0:T(8,128)S(1)} %collective-permute-done.10), channel_id=1, source_target_pairs={{0,28},{4,0},{8,4},{12,8},{16,12},{20,16},{24,20},{28,24},{1,29},{... | collective-permute-start | bytes 393224 | tf_op jit(solution)/shard_map/ppermute | solution.py:20
  403.4 7.7 %collective-permute-start.13 = (f32[1,1,256,128]{2,3,1,0:T(8,128)S(1)}, f32[1,1,256,128]{2,3,1,0:T(8,128)S(1)}, u32[]{:S(2)}, u32[]{:S(2)}) collective-permute-start(f32[1,1,256,128]{2,3,1,0:T(8,128)S(1)} %collective-permute-done.11), channel_id=1, source_target_pairs={{0,4},{4,8},{8,12},{12,16},{16,20},{20,24},{24,28},{28,0},{1,5},{5... | collective-permute-start | bytes 393224 | tf_op jit(solution)/shard_map/ppermute | solution.py:17
  413.4 1.2 copy-start
  (2 other events, 2.1 us)
Sparse Core Ops, SparseCore 0:
  10.7 73.7 all-reduce.6
  148.4 17.0 all-reduce.8
  200.1 22.2 all-reduce.10
  225.6 71.0 all-reduce.12
  361.6 17.0 all-reduce.14
  413.6 17.7 reduce-scatter.1
